TPU v7x, 512 devices: a whole 4x8x8 slice. The times are simulated.
512 devices in a mesh: tick: 64 (over y, z_hi, core), wire: 8 (over z_lo, x).
Axes of the slice: x: 4, y: 8, z: 8 (z_hi: 4, z_lo: 2; z = z_hi * 2 + z_lo), core: 2. Of those that a mesh axis runs over, the one named last changes fastest.
Arguments:
- signal: float32 [16, 512, 8192], P(None, 'wire', 'tick'), may hold values from -6 to 6
- kernel_front: float32 [16, 3, 9], replicated, may hold values from -1.25 to 1.25
- mixing_front: float32 [16, 16], replicated, may hold values from -1.5 to 1.5
- offset_front: float32 [16], replicated, may hold values from -2 to 2
- kernel_back: float32 [16, 3, 9], replicated, may hold values from -1.25 to 1.25
- mixing_back: float32 [16, 16], replicated, may hold values from -1.5 to 1.5
- offset_back: float32 [16], replicated, may hold values from -2 to 2
- upstream: float32 [16, 512, 8192], P(None, 'wire', 'tick'), may hold values from -13 to 13
Outputs:
- response: float32 [16, 512, 8192], P(None, 'wire', 'tick')
- signal_grad: float32 [16, 512, 8192], P(None, 'wire', 'tick')
- kernel_front_grad: float32 [16, 3, 9], replicated
- mixing_front_grad: float32 [16, 16], replicated
- offset_front_grad: float32 [16], replicated
- kernel_back_grad: float32 [16, 3, 9], replicated
- mixing_back_grad: float32 [16, 16], replicated
- offset_back_grad: float32 [16], replicated
All inputs are finite; a program needn't handle non-finite values.
Results may differ from a plain program's by a relative error of at most 0.0003.
Values sent between devices are 32-bit elements; how exact they have to be, the bound alone decides.
No kernel may reach another device: no remote copies, remote signals or barrier semaphores. Data moves between devices by JAX's collectives and lax.ppermute only.
A program may use at most 64 MiB of HBM per device.

v0:
```python
import math
import jax
import jax.numpy as jnp
from jax import lax
from jax.sharding import Mesh, PartitionSpec as P

TICK_DILATION = 8
TICK = ("y", "z_hi", "core")
WIRE = ("z_lo", "x")
REDUCTION_ORDER = ("core", "x", ("z_hi", "z_lo"), "y")


def with_halo(block, sides, width):
    for axis, dim in sides:
        count = lax.axis_size(axis)
        forward = [(i, i + 1) for i in range(count - 1)]
        backward = [(target, source) for source, target in forward]
        low = lax.ppermute(
            lax.slice_in_dim(block, block.shape[dim] - width, None, axis=dim), axis, forward
        )
        high = lax.ppermute(lax.slice_in_dim(block, 0, width, axis=dim), axis, backward)
        block = jnp.concatenate([low, block, high], axis=dim)
    return block


def spread(field, tick_deep, wire_deep):
    longer = with_halo(field, ((TICK, 2),), tick_deep)
    return with_halo(longer, ((WIRE, 1),), wire_deep)


def depthwise(padded_input, kernel_weight, row_count, column_count):
    total_sum = jnp.zeros((padded_input.shape[0], row_count, column_count), jnp.float32)
    for row_index in range(3):
        for column_index in range(9):
            total_sum = (
                total_sum
                + kernel_weight[:, row_index, column_index][:, None, None]
                * padded_input[
                    :,
                    row_index : row_index + row_count,
                    TICK_DILATION * column_index : TICK_DILATION * column_index + column_count,
                ]
            )
    return total_sum


def tap_grads(upward_gradient, padded_input):
    row_count = upward_gradient.shape[1]
    column_count = upward_gradient.shape[2]
    text_lines = []
    for row_index in range(3):
        text_lines.append(
            jnp.stack(
                [
                    jnp.sum(
                        upward_gradient
                        * padded_input[
                            :,
                            row_index : row_index + row_count,
                            TICK_DILATION * column_index : TICK_DILATION * column_index
                            + column_count,
                        ],
                        axis=(1, 2),
                    )
                    for column_index in range(9)
                ],
                axis=1,
            )
        )
    return jnp.stack(text_lines, axis=1)


def mixing(matrix, field, offset):
    return (
        jnp.einsum("oc,cwt->owt", matrix, field, precision=lax.Precision.HIGHEST)
        + offset[:, None, None]
    )


def slope(preact):
    sig = jax.nn.sigmoid(preact)
    return sig * (1.0 + preact * (1.0 - sig))


def per_device(
    signal,
    kernel_front,
    mixing_front,
    offset_front,
    kernel_back,
    mixing_back,
    offset_back,
    upstream,
):
    row_count = signal.shape[1]
    column_count = signal.shape[2]
    kernel_extent = 4 * TICK_DILATION
    padded_in = spread(signal, kernel_extent, 1)
    taps_front = depthwise(padded_in, kernel_front, row_count, column_count)
    pre_front = mixing(mixing_front, taps_front, offset_front)
    padded_act = spread(jax.nn.silu(pre_front), kernel_extent, 1)
    taps_back = depthwise(padded_act, kernel_back, row_count, column_count)
    pre_back = mixing(mixing_back, taps_back, offset_back)
    response = jax.nn.silu(pre_back)
    grad_back = upstream * slope(pre_back)
    gmix_back = jnp.einsum("owt,cwt->oc", grad_back, taps_back, precision=lax.Precision.HIGHEST)
    gbias_back = jnp.sum(grad_back, axis=(1, 2))
    under_back = jnp.einsum("oc,owt->cwt", mixing_back, grad_back, precision=lax.Precision.HIGHEST)
    gkern_back = tap_grads(under_back, padded_act)
    into_front = depthwise(
        spread(under_back, kernel_extent, 1), kernel_back[:, ::-1, ::-1], row_count, column_count
    )
    grad_front = into_front * slope(pre_front)
    gmix_front = jnp.einsum("owt,cwt->oc", grad_front, taps_front, precision=lax.Precision.HIGHEST)
    gbias_front = jnp.sum(grad_front, axis=(1, 2))
    under_front = jnp.einsum(
        "oc,owt->cwt", mixing_front, grad_front, precision=lax.Precision.HIGHEST
    )
    gkern_front = tap_grads(under_front, padded_in)
    signal_grad = depthwise(
        spread(under_front, kernel_extent, 1), kernel_front[:, ::-1, ::-1], row_count, column_count
    )
    totals = (gkern_front, gmix_front, gbias_front, gkern_back, gmix_back, gbias_back)
    packed = jnp.concatenate([item.reshape(-1) for item in totals])
    for group in REDUCTION_ORDER:
        packed = lax.psum(packed, group)
    sizes = [math.prod(item.shape) for item in totals]
    pieces = jnp.split(packed, [sum(sizes[: k + 1]) for k in range(len(sizes) - 1)])
    totals = [piece.reshape(item.shape) for piece, item in zip(pieces, totals)]
    factor = 1.0 / math.sqrt(row_count * lax.axis_size(WIRE) * column_count * lax.axis_size(TICK))
    return (
        response,
        signal_grad,
        totals[0] * factor,
        totals[1] * factor,
        totals[2] * factor,
        totals[3] * factor,
        totals[4] * factor,
        totals[5] * factor,
    )


def solution(mesh):
    fine = Mesh(mesh.devices.reshape(8, 4, 2, 2, 4), TICK + WIRE)
    block = P(None, WIRE, TICK)
    in_specs = (block, P(), P(), P(), P(), P(), P(), block)
    out_specs = (block, block, P(), P(), P(), P(), P(), P())
    return jax.shard_map(
        per_device, mesh=fine, in_specs=in_specs, out_specs=out_specs, check_vma=False
    )
```

profile of v0, /device:TPU:27, one launch (start us, length us, event | category | flops | bytes accessed | tf_op | source)
XLA Modules:
  0.0 215.1 jit_solution(8928391900136740163)
XLA Ops:
  2.2 6.4 %collective-permute-start = (f32[16,64,32]{2,0,1:T(8,128)S(1)}, f32[16,64,32]{2,0,1:T(8,128)S(1)}, u32[]{:S(2)}, u32[]{:S(2)}) collective-permute-start(f32[16,64,32]{2,0,1:T(8,128)S(1)} %get-tuple-element.133), channel_id=1, source_target_pairs={{0,8},{8,16},{16,24},{24,32},{32,40},{40,48},{48,56},{56,64},{64,7... | collective-permute-start | bytes 393224 | tf_op jit(solution)/shard_map/ppermute | solution.py:18
  10.6 5.6 %collective-permute-done = f32[16,64,32]{2,0,1:T(8,128)S(1)} collective-permute-done((f32[16,64,32]{2,0,1:T(8,128)S(1)}, f32[16,64,32]{2,0,1:T(8,128)S(1)}, u32[]{:S(2)}, u32[]{:S(2)}) %collective-permute-start) | collective-permute-done | bytes 131104 | tf_op jit(solution)/shard_map/ppermute | solution.py:18
  16.2 12.0 %collective-permute-done.1 = f32[16,64,32]{2,0,1:T(8,128)S(1)} collective-permute-done((f32[16,64,32]{2,0,1:T(8,128)S(1)}, f32[16,64,32]{2,0,1:T(8,128)S(1)}, u32[]{:S(2)}, u32[]{:S(2)}) %collective-permute-start.1) | collective-permute-done | bytes 131104 | tf_op jit(solution)/shard_map/ppermute | solution.py:21
  28.3 3.1 %collective-permute-start.2 = (f32[16,1,192]{2,0,1:T(8,128)S(1)}, f32[16,1,192]{2,0,1:T(8,128)S(1)}, u32[]{:S(2)}, u32[]{:S(2)}) collective-permute-start(f32[16,1,192]{2,0,1:T(8,128)S(1)} %get-tuple-element.122), channel_id=1, source_target_pairs={{0,1},{1,2},{2,3},{3,4},{4,5},{5,6},{6,7},{8,9},{9,10},{10,11},{11... | collective-permute-start | bytes 36872 | tf_op jit(solution)/shard_map/ppermute | solution.py:18
  36.8 3.9 %multiply_add_fusion.1 = f32[16,64,128]{2,0,1:T(8,128)S(1)} fusion(f32[16,64,128]{2,0,1:T(8,128)S(1)} %get-tuple-element.132, f32[16,65,192]{2,0,1:T(8,128)S(1)} %get-tuple-element.121, f32[16,64,160]{2,0,1:T(8,128)S(1)} %constant_dynamic-update-slice_fusion, f32[16,65,192]{2,0,1:T(8,128)S(1)} %get-tuple-element.120, f32[16]{0:T(128)S(1)} %get-tuple-element.187, ...), kind=kLoop, calls=%fused_computation.251 | loop fusion | flops 7471104 | bytes 12715712 | tf_op jit(solution)/shard_map/add | solution.py:36
  46.8 6.7 %collective-permute-done.4 = f32[16,64,32]{2,0,1:T(8,128)S(1)} collective-permute-done((f32[16,64,32]{2,0,1:T(8,128)S(1)}, f32[16,64,32]{2,0,1:T(8,128)S(1)}, u32[]{:S(2)}, u32[]{:S(2)}) %collective-permute-start.4) | collective-permute-done | bytes 131104 | tf_op jit(solution)/shard_map/ppermute | solution.py:18
  53.5 9.8 %collective-permute-done.5 = f32[16,64,32]{2,0,1:T(8,128)S(1)} collective-permute-done((f32[16,64,32]{2,0,1:T(8,128)S(1)}, f32[16,64,32]{2,0,1:T(8,128)S(1)}, u32[]{:S(2)}, u32[]{:S(2)}) %collective-permute-start.5) | collective-permute-done | bytes 131104 | tf_op jit(solution)/shard_map/ppermute | solution.py:21
  63.3 4.9 %collective-permute-start.6 = (f32[16,1,192]{2,0,1:T(8,128)S(1)}, f32[16,1,192]{2,0,1:T(8,128)S(1)}, u32[]{:S(2)}, u32[]{:S(2)}) collective-permute-start(f32[16,1,192]{2,0,1:T(8,128)S(1)} %get-tuple-element.118), channel_id=1, source_target_pairs={{0,1},{1,2},{2,3},{3,4},{4,5},{5,6},{6,7},{8,9},{9,10},{10,11},{11... | collective-permute-start | bytes 36872 | tf_op jit(solution)/shard_map/ppermute | solution.py:18
  70.2 2.5 %collective-permute-done.7 = f32[16,1,192]{2,0,1:T(8,128)S(1)} collective-permute-done((f32[16,1,192]{2,0,1:T(8,128)S(1)}, f32[16,1,192]{2,0,1:T(8,128)S(1)}, u32[]{:S(2)}, u32[]{:S(2)}) %collective-permute-start.7) | collective-permute-done | bytes 12320 | tf_op jit(solution)/shard_map/ppermute | solution.py:21
  73.7 4.5 %multiply_add_fusion = f32[16,64,128]{2,0,1:T(8,128)S(1)} fusion(f32[16,64,128]{2,0,1:T(8,128)S(1)} %get-tuple-element.195, f32[16,65,192]{2,0,1:T(8,128)S(1)} %get-tuple-element.117, f32[16,65,192]{2,0,1:T(8,128)S(1)} %get-tuple-element.116, f32[16]{0:T(128)S(1)} %get-tuple-element.160, f32[16]{0:T(128)S(1)} %get-tuple-element.161, ...), kind=kLoop, calls=%fused_computation.248 | loop fusion | flops 7995392 | bytes 10749632 | tf_op jit(solution)/shard_map/add | solution.py:36
  80.0 3.0 %multiply_reduce_fusion.18 = (f32[16]{0:T(128)S(1)}, f32[16]{0:T(128)S(1)}, f32[16]{0:T(128)S(1)}, f32[16]{0:T(128)S(1)}, f32[16]{0:T(128)S(1)}, /*index=5*/f32[...) fusion(f32[16,65,192]{2,0,1:T(8,128)S(1)} %get-tuple-element.11, ...), kind=kOutput, calls=%fused_computation.210 | convolution fusion | flops 29884128 | bytes 10487936 | tf_op jit(solution)/shard_map/oc,owt->cwt/dot_general | solution.py:108
  88.8 5.1 %multiply_reduce_fusion.9 = (f32[16]{0:T(128)S(1)}, f32[16]{0:T(128)S(1)}, f32[16]{0:T(128)S(1)}, f32[16]{0:T(128)S(1)}, f32[16]{0:T(128)S(1)}, /*index=5*/f32[1...) fusion(f32[16,64,128]{2,0,1:T(8,128)} %copy-done.3, f32[16,64,32]{2,0,1:T(8,128)} %copy-done.8, ...), kind=kLoop, calls=%fused_computation.201 | loop fusion | flops 3932016 | bytes 1835584 | tf_op jit(solution)/shard_map/reduce_sum | solution.py:55
  98.5 8.5 %collective-permute-done.9 = f32[16,64,32]{2,0,1:T(8,128)} collective-permute-done((f32[16,64,32]{2,0,1:T(8,128)}, f32[16,64,32]{2,0,1:T(8,128)}, u32[]{:S(2)}, u32[]{:S(2)}) %collective-permute-start.9) | collective-permute-done | bytes 131104 | tf_op jit(solution)/shard_map/ppermute | solution.py:21
  110.0 3.0 %collective-permute-start.11 = (f32[16,1,192]{2,0,1:T(8,128)S(1)}, f32[16,1,192]{2,0,1:T(8,128)S(1)}, u32[]{:S(2)}, u32[]{:S(2)}) collective-permute-start(f32[16,1,192]{2,0,1:T(8,128)S(1)} %get-tuple-element.115), channel_id=1, source_target_pairs={{1,0},{2,1},{3,2},{4,3},{5,4},{6,5},{7,6},{9,8},{10,9},{11,10},{12... | collective-permute-start | bytes 36872 | tf_op jit(solution)/shard_map/ppermute | solution.py:21
  117.9 6.5 %fusion.99 = (f32[16]{0:T(128)S(1)}, f32[16,64,128]{2,0,1:T(8,128)S(1)}) fusion(f32[16,64,128]{2,0,1:T(8,128)S(1)} %copy-done.13, f32[16,65,192]{2,0,1:T(8,128)S(1)} %get-tuple-element.113, f32[16]{0:T(128)S(1)} %get-tuple-element.135, f32[16]{0:T(128)S(1)} %get-tuple-element.154, f32[16]{0:T(128)S(1)} %get-tuple-element.159, f32[16]{0:T(128)S(1)} %get-tuple-element.158, ...), kind=kLoop, calls=%fused_computation.333 | loop fusion | flops 9175024 | bytes 11273984 | tf_op jit(solution)/shard_map/reduce_sum | solution.py:115
  125.2 3.0 %multiply_reduce_fusion.45 = (f32[16]{0:T(128)S(1)}, f32[16]{0:T(128)S(1)}, f32[16]{0:T(128)S(1)}, f32[16]{0:T(128)S(1)}, f32[16]{0:T(128)S(1)}, /*index=5*/f32[...) fusion(f32[16,65,192]{2,0,1:T(8,128)S(1)} %get-tuple-element.12, ...), kind=kOutput, calls=%fused_computation.237 | convolution fusion | flops 29884128 | bytes 10487936 | tf_op jit(solution)/shard_map/oc,owt->cwt/dot_general | solution.py:116
  135.0 6.2 %psum.29 = f32[1408]{0:T(1024)S(1)} all-reduce(f32[1408]{0:T(1024)S(1)} %psum.28), channel_id=1, replica_groups=mesh['y'=8,'z_hi'=4,'core'=2,'z_lo'=2,'x'=4] {'x'}, use_global_device_ids=true, to_apply=%region_57.58 | all-reduce | flops 1408 | bytes 11264 | tf_op jit(solution)/shard_map/psum | solution.py:126
  141.2 15.5 %psum.30 = f32[1408]{0:T(1024)S(1)} all-reduce(f32[1408]{0:T(1024)S(1)} %psum.29), channel_id=1, replica_groups=mesh['y'=8,'z_hi'=4,'core'=2,'z_lo'=2,'x'=4] {'z_hi','z_lo'}, use_global_device_ids=true, to_apply=%region_58.59 | all-reduce | flops 1408 | bytes 11264 | tf_op jit(solution)/shard_map/psum | solution.py:126
  156.7 10.7 %psum.31 = f32[1408]{0:T(1024)S(1)} all-reduce(f32[1408]{0:T(1024)S(1)} %psum.30), channel_id=1, replica_groups=mesh['y'=8,'z_hi'=4,'core'=2,'z_lo'=2,'x'=4] {'y'}, use_global_device_ids=true, to_apply=%region_59.60 | all-reduce | flops 1408 | bytes 11264 | tf_op jit(solution)/shard_map/psum | solution.py:126
  167.5 11.2 %collective-permute-start.12 = (f32[16,64,32]{2,0,1:T(8,128)}, f32[16,64,32]{2,0,1:T(8,128)S(1)}, u32[]{:S(2)}, u32[]{:S(2)}) collective-permute-start(f32[16,64,32]{2,0,1:T(8,128)} %get-tuple-element.124), channel_id=1, source_target_pairs={{0,8},{8,16},{16,24},{24,32},{32,40},{40,48},{48,56},{56,64},{64,7... | collective-permute-start | bytes 393224 | tf_op jit(solution)/shard_map/ppermute | solution.py:18
  180.8 9.9 %collective-permute-done.12 = f32[16,64,32]{2,0,1:T(8,128)S(1)} collective-permute-done((f32[16,64,32]{2,0,1:T(8,128)}, f32[16,64,32]{2,0,1:T(8,128)S(1)}, u32[]{:S(2)}, u32[]{:S(2)}) %collective-permute-start.12) | collective-permute-done | bytes 131104 | tf_op jit(solution)/shard_map/ppermute | solution.py:18
  190.7 8.8 %collective-permute-done.13 = f32[16,64,32]{2,0,1:T(8,128)S(1)} collective-permute-done((f32[16,64,32]{2,0,1:T(8,128)}, f32[16,64,32]{2,0,1:T(8,128)S(1)}, u32[]{:S(2)}, u32[]{:S(2)}) %collective-permute-start.13) | collective-permute-done | bytes 131104 | tf_op jit(solution)/shard_map/ppermute | solution.py:21
  201.5 3.6 %collective-permute-start.15 = (f32[16,1,192]{2,0,1:T(8,128)S(1)}, f32[16,1,192]{2,0,1:T(8,128)S(1)}, u32[]{:S(2)}, u32[]{:S(2)}) collective-permute-start(f32[16,1,192]{2,0,1:T(8,128)S(1)} %get-tuple-element.111), channel_id=1, source_target_pairs={{1,0},{2,1},{3,2},{4,3},{5,4},{6,5},{7,6},{9,8},{10,9},{11,10},{12... | collective-permute-start | bytes 36872 | tf_op jit(solution)/shard_map/ppermute | solution.py:21
  209.6 4.5 %fusion.14 = f32[16,64,128]{2,0,1:T(8,128)S(1)} fusion(f32[16,64,128]{2,0,1:T(8,128)S(1)} %get-tuple-element.197, f32[16,64,32]{2,0,1:T(8,128)S(1)} %collective-permute-done.13, f32[16,64,32]{2,0,1:T(8,128)S(1)} %collective-permute-done.12, f32[16,65,192]{2,0,1:T(8,128)S(1)} %get-tuple-element.109, f32[16,65,192]{2,0,1:T(8,128)S(1)} %get-tuple-element.108, ...), kind=kLoop, calls=%fused_computation.70 | loop fusion | flops 7995392 | bytes 10749632 | tf_op jit(solution)/shard_map/add | solution.py:36
  (110 shorter events, 55.0 us)
Async XLA Ops:
  0.6 77.5 %copy-start = (f32[16,16]{1,0:T(8,128)S(1)}, f32[16,16]{1,0:T(8,128)}, u32[]{:S(2)}) copy-start(f32[16,16]{1,0:T(8,128)} %param.13) | copy-start | bytes 3076
  2.0 8.5 %copy-start.15 = (f32[16,3,9]{0,1,2:T(4,128)S(1)}, f32[16,3,9]{0,1,2:T(4,128)}, u32[]{:S(2)}) copy-start(f32[16,3,9]{0,1,2:T(4,128)} %param.9) | copy-start | bytes 5188
  2.2 14.0 %collective-permute-start = (f32[16,64,32]{2,0,1:T(8,128)S(1)}, f32[16,64,32]{2,0,1:T(8,128)S(1)}, u32[]{:S(2)}, u32[]{:S(2)}) collective-permute-start(f32[16,64,32]{2,0,1:T(8,128)S(1)} %get-tuple-element.133), channel_id=1, source_target_pairs={{0,8},{8,16},{16,24},{24,32},{32,40},{40,48},{48,56},{56,64},{64,7... | collective-permute-start | bytes 393224 | tf_op jit(solution)/shard_map/ppermute | solution.py:18
  8.6 19.6 %collective-permute-start.1 = (f32[16,64,32]{2,0,1:T(8,128)S(1)}, f32[16,64,32]{2,0,1:T(8,128)S(1)}, u32[]{:S(2)}, u32[]{:S(2)}) collective-permute-start(f32[16,64,32]{2,0,1:T(8,128)S(1)} %get-tuple-element.134), channel_id=1, source_target_pairs={{8,0},{16,8},{24,16},{32,24},{40,32},{48,40},{56,48},{64,56},{72,6... | collective-permute-start | bytes 393224 | tf_op jit(solution)/shard_map/ppermute | solution.py:21
  16.2 20.5 %copy-start.5 = (f32[16,64,32]{2,0,1:T(8,128)}, f32[16,64,32]{2,0,1:T(8,128)S(1)}, u32[]{:S(2)}) copy-start(f32[16,64,32]{2,0,1:T(8,128)S(1)} %collective-permute-done) | copy-start | bytes 393220
  28.3 5.4 %collective-permute-start.2 = (f32[16,1,192]{2,0,1:T(8,128)S(1)}, f32[16,1,192]{2,0,1:T(8,128)S(1)}, u32[]{:S(2)}, u32[]{:S(2)}) collective-permute-start(f32[16,1,192]{2,0,1:T(8,128)S(1)} %get-tuple-element.122), channel_id=1, source_target_pairs={{0,1},{1,2},{2,3},{3,4},{4,5},{5,6},{6,7},{8,9},{9,10},{10,11},{11... | collective-permute-start | bytes 36872 | tf_op jit(solution)/shard_map/ppermute | solution.py:18
  31.4 4.5 %collective-permute-start.3 = (f32[16,1,192]{2,0,1:T(8,128)S(1)}, f32[16,1,192]{2,0,1:T(8,128)S(1)}, u32[]{:S(2)}, u32[]{:S(2)}) collective-permute-start(f32[16,1,192]{2,0,1:T(8,128)S(1)} %get-tuple-element.123), channel_id=1, source_target_pairs={{1,0},{2,1},{3,2},{4,3},{5,4},{6,5},{7,6},{9,8},{10,9},{11,10},{12... | collective-permute-start | bytes 36872 | tf_op jit(solution)/shard_map/ppermute | solution.py:21
  42.4 11.1 %collective-permute-start.4 = (f32[16,64,32]{2,0,1:T(8,128)S(1)}, f32[16,64,32]{2,0,1:T(8,128)S(1)}, u32[]{:S(2)}, u32[]{:S(2)}) collective-permute-start(f32[16,64,32]{2,0,1:T(8,128)S(1)} %get-tuple-element.129), channel_id=1, source_target_pairs={{0,8},{8,16},{16,24},{24,32},{32,40},{40,48},{48,56},{56,64},{64,7... | collective-permute-start | bytes 393224 | tf_op jit(solution)/shard_map/ppermute | solution.py:18
  44.6 18.7 %collective-permute-start.5 = (f32[16,64,32]{2,0,1:T(8,128)S(1)}, f32[16,64,32]{2,0,1:T(8,128)S(1)}, u32[]{:S(2)}, u32[]{:S(2)}) collective-permute-start(f32[16,64,32]{2,0,1:T(8,128)S(1)} %get-tuple-element.130), channel_id=1, source_target_pairs={{8,0},{16,8},{24,16},{32,24},{40,32},{48,40},{56,48},{64,56},{72,6... | collective-permute-start | bytes 393224 | tf_op jit(solution)/shard_map/ppermute | solution.py:21
  53.5 20.1 %copy-start.7 = (f32[16,64,32]{2,0,1:T(8,128)}, f32[16,64,32]{2,0,1:T(8,128)S(1)}, u32[]{:S(2)}) copy-start(f32[16,64,32]{2,0,1:T(8,128)S(1)} %collective-permute-done.4) | copy-start | bytes 393220
  63.3 10.4 %copy-start.8 = (f32[16,64,32]{2,0,1:T(8,128)}, f32[16,64,32]{2,0,1:T(8,128)S(1)}, u32[]{:S(2)}) copy-start(f32[16,64,32]{2,0,1:T(8,128)S(1)} %collective-permute-done.5) | copy-start | bytes 393220
  63.3 6.9 %collective-permute-start.6 = (f32[16,1,192]{2,0,1:T(8,128)S(1)}, f32[16,1,192]{2,0,1:T(8,128)S(1)}, u32[]{:S(2)}, u32[]{:S(2)}) collective-permute-start(f32[16,1,192]{2,0,1:T(8,128)S(1)} %get-tuple-element.118), channel_id=1, source_target_pairs={{0,1},{1,2},{2,3},{3,4},{4,5},{5,6},{6,7},{8,9},{9,10},{10,11},{11... | collective-permute-start | bytes 36872 | tf_op jit(solution)/shard_map/ppermute | solution.py:18
  68.3 4.5 %collective-permute-start.7 = (f32[16,1,192]{2,0,1:T(8,128)S(1)}, f32[16,1,192]{2,0,1:T(8,128)S(1)}, u32[]{:S(2)}, u32[]{:S(2)}) collective-permute-start(f32[16,1,192]{2,0,1:T(8,128)S(1)} %get-tuple-element.119), channel_id=1, source_target_pairs={{1,0},{2,1},{3,2},{4,3},{5,4},{6,5},{7,6},{9,8},{10,9},{11,10},{12... | collective-permute-start | bytes 36872 | tf_op jit(solution)/shard_map/ppermute | solution.py:21
  83.1 5.7 %copy-start.3 = (f32[16,64,128]{2,0,1:T(8,128)}, f32[16,64,128]{2,0,1:T(8,128)S(1)}, u32[]{:S(2)}) copy-start(f32[16,64,128]{2,0,1:T(8,128)S(1)} %get-tuple-element.198) | copy-start | bytes 1572868
  84.2 14.2 %collective-permute-start.8 = (f32[16,64,32]{2,0,1:T(8,128)}, f32[16,64,32]{2,0,1:T(8,128)}, u32[]{:S(2)}, u32[]{:S(2)}) collective-permute-start(f32[16,64,32]{2,0,1:T(8,128)} %get-tuple-element.126), channel_id=1, source_target_pairs={{0,8},{8,16},{16,24},{24,32},{32,40},{40,48},{48,56},{56,64},{64,7... | collective-permute-start | bytes 393224 | tf_op jit(solution)/shard_map/ppermute | solution.py:18
  86.4 20.5 %collective-permute-start.9 = (f32[16,64,32]{2,0,1:T(8,128)}, f32[16,64,32]{2,0,1:T(8,128)}, u32[]{:S(2)}, u32[]{:S(2)}) collective-permute-start(f32[16,64,32]{2,0,1:T(8,128)} %get-tuple-element.127), channel_id=1, source_target_pairs={{8,0},{16,8},{24,16},{32,24},{40,32},{48,40},{56,48},{64,56},{72,6... | collective-permute-start | bytes 393224 | tf_op jit(solution)/shard_map/ppermute | solution.py:21
  93.9 13.1 %copy-start.4 = (f32[16,64,128]{2,0,1:T(8,128)S(1)}, f32[16,64,128]{2,0,1:T(8,128)}, u32[]{:S(2)}) copy-start(f32[16,64,128]{2,0,1:T(8,128)} %copy-done.3) | copy-start | bytes 1572868
  107.8 7.6 %collective-permute-start.10 = (f32[16,1,192]{2,0,1:T(8,128)S(1)}, f32[16,1,192]{2,0,1:T(8,128)S(1)}, u32[]{:S(2)}, u32[]{:S(2)}) collective-permute-start(f32[16,1,192]{2,0,1:T(8,128)S(1)} %get-tuple-element.114), channel_id=1, source_target_pairs={{0,1},{1,2},{2,3},{3,4},{4,5},{5,6},{6,7},{8,9},{9,10},{10,11},{11... | collective-permute-start | bytes 36872 | tf_op jit(solution)/shard_map/ppermute | solution.py:18
  110.0 5.4 %collective-permute-start.11 = (f32[16,1,192]{2,0,1:T(8,128)S(1)}, f32[16,1,192]{2,0,1:T(8,128)S(1)}, u32[]{:S(2)}, u32[]{:S(2)}) collective-permute-start(f32[16,1,192]{2,0,1:T(8,128)S(1)} %get-tuple-element.115), channel_id=1, source_target_pairs={{1,0},{2,1},{3,2},{4,3},{5,4},{6,5},{7,6},{9,8},{10,9},{11,10},{12... | collective-permute-start | bytes 36872 | tf_op jit(solution)/shard_map/ppermute | solution.py:21
  117.9 6.5 %copy-start.11 = (f32[16,64,128]{2,0,1:T(8,128)S(1)}, f32[16,64,128]{2,0,1:T(8,128)}, u32[]{:S(2)}) copy-start(f32[16,64,128]{2,0,1:T(8,128)} %copy-done.10) | copy-start | bytes 1572868
  167.5 23.2 %collective-permute-start.12 = (f32[16,64,32]{2,0,1:T(8,128)}, f32[16,64,32]{2,0,1:T(8,128)S(1)}, u32[]{:S(2)}, u32[]{:S(2)}) collective-permute-start(f32[16,64,32]{2,0,1:T(8,128)} %get-tuple-element.124), channel_id=1, source_target_pairs={{0,8},{8,16},{16,24},{24,32},{32,40},{40,48},{48,56},{56,64},{64,7... | collective-permute-start | bytes 393224 | tf_op jit(solution)/shard_map/ppermute | solution.py:18
  178.6 20.9 %collective-permute-start.13 = (f32[16,64,32]{2,0,1:T(8,128)}, f32[16,64,32]{2,0,1:T(8,128)S(1)}, u32[]{:S(2)}, u32[]{:S(2)}) collective-permute-start(f32[16,64,32]{2,0,1:T(8,128)} %get-tuple-element.125), channel_id=1, source_target_pairs={{8,0},{16,8},{24,16},{32,24},{40,32},{48,40},{56,48},{64,56},{72,6... | collective-permute-start | bytes 393224 | tf_op jit(solution)/shard_map/ppermute | solution.py:21
  199.6 9.2 %collective-permute-start.14 = (f32[16,1,192]{2,0,1:T(8,128)S(1)}, f32[16,1,192]{2,0,1:T(8,128)S(1)}, u32[]{:S(2)}, u32[]{:S(2)}) collective-permute-start(f32[16,1,192]{2,0,1:T(8,128)S(1)} %get-tuple-element.110), channel_id=1, source_target_pairs={{0,1},{1,2},{2,3},{3,4},{4,5},{5,6},{6,7},{8,9},{9,10},{10,11},{11... | collective-permute-start | bytes 36872 | tf_op jit(solution)/shard_map/ppermute | solution.py:18
  201.5 7.2 %collective-permute-start.15 = (f32[16,1,192]{2,0,1:T(8,128)S(1)}, f32[16,1,192]{2,0,1:T(8,128)S(1)}, u32[]{:S(2)}, u32[]{:S(2)}) collective-permute-start(f32[16,1,192]{2,0,1:T(8,128)S(1)} %get-tuple-element.111), channel_id=1, source_target_pairs={{1,0},{2,1},{3,2},{4,3},{5,4},{6,5},{7,6},{9,8},{10,9},{11,10},{12... | collective-permute-start | bytes 36872 | tf_op jit(solution)/shard_map/ppermute | solution.py:21
  (13 other events, 38.7 us)
where the time goes:
time: 216 us; the launch traced here: 215 us
  waiting for transfers between devices  68.6 us (32%)
  starting transfers between devices  53.2 us (25%)
  blocking collectives  34.9 us (16%)
  other arithmetic  33.2 us (15%)
  matrix products  12.1 us (6%)
  local copies, waits for them, and re-layouts  11.9 us (6%)
    ppermute x8, waiting for transfers between devices, with_halo(): lax.ppermute(lax.slice_in_dim(block, 0, width, axis=dim), axis, backward)  43.7 us
    psum x4, blocking collectives, per_device(): packed = lax.psum(packed, group)  34.9 us
    ppermute x8, starting transfers between devices, with_halo(): lax.ppermute(lax.slice_in_dim(block, block.shape[dim] - width, None, axis...  34.1 us
    ppermute x8, waiting for transfers between devices, with_halo(): lax.ppermute(lax.slice_in_dim(block, block.shape[dim] - width, None, axis...  24.8 us
    ppermute x8, starting transfers between devices, with_halo(): lax.ppermute(lax.slice_in_dim(block, 0, width, axis=dim), axis, backward)  19.2 us
    add x3, other arithmetic, depthwise(): total_sum + kernel_weight[:, row_index, column_index][:, None, None] * pa...  12.9 us
    reduce_sum x2, other arithmetic, tap_grads(): jnp.sum(upward_gradient * padded_input[:, row_index:row_index + row_count...  6.91 us
    unnamed x47, local copies, waits for them, and re-layouts  6.58 us
  transfers between devices with their start and end apart: 16, of which 10 were waited for; matrix products, arithmetic and copies ran while one was open for 6% of the time, Pallas kernels for 0%

commit v1 on v0

--- a/solution.py
+++ b/solution.py
@@ -123,7 +123,7 @@
     totals = (gkern_front, gmix_front, gbias_front, gkern_back, gmix_back, gbias_back)
     packed = jnp.concatenate([item.reshape(-1) for item in totals])
     for group in REDUCTION_ORDER:
-        packed = lax.psum(packed, group)
+        packed = jnp.sum(lax.all_gather(packed, group), axis=0)
     sizes = [math.prod(item.shape) for item in totals]
     pieces = jnp.split(packed, [sum(sizes[: k + 1]) for k in range(len(sizes) - 1)])
     totals = [piece.reshape(item.shape) for piece, item in zip(pieces, totals)]

time: 216 us -> 237 us (1.097)
  the two profiles are of different devices: /device:TPU:27 before, /device:TPU:89 now
where the time goes in v1:
time: 237 us; the launch traced here: 236 us
  starting transfers between devices  73.9 us (31%)
  waiting for transfers between devices  51.6 us (22%)
  blocking collectives  50.6 us (21%)
  other arithmetic  34.6 us (15%)
  matrix products  12.1 us (5%)
  local copies, waits for them, and re-layouts  11.9 us (5%)
    all_gather x4, blocking collectives, per_device(): packed = jnp.sum(lax.all_gather(packed, group), axis=0)  50.6 us
    ppermute x8, starting transfers between devices, with_halo(): lax.ppermute(lax.slice_in_dim(block, block.shape[dim] - width, None, axis...  37.2 us
    ppermute x8, starting transfers between devices, with_halo(): lax.ppermute(lax.slice_in_dim(block, 0, width, axis=dim), axis, backward)  36.7 us
    ppermute x8, waiting for transfers between devices, with_halo(): lax.ppermute(lax.slice_in_dim(block, block.shape[dim] - width, None, axis...  30.1 us
    ppermute x8, waiting for transfers between devices, with_halo(): lax.ppermute(lax.slice_in_dim(block, 0, width, axis=dim), axis, backward)  21.5 us
    add x3, other arithmetic, depthwise(): total_sum + kernel_weight[:, row_index, column_index][:, None, None] * pa...  12.9 us
    reduce_sum x2, other arithmetic, tap_grads(): jnp.sum(upward_gradient * padded_input[:, row_index:row_index + row_count...  6.91 us
    unnamed x55, local copies, waits for them, and re-layouts  6.61 us
  transfers between devices with their start and end apart: 16, of which 10 were waited for; matrix products, arithmetic and copies ran while one was open for 6% of the time, Pallas kernels for 0%

profile of v1, /device:TPU:89, one launch (start us, length us, event | category | flops | bytes accessed | tf_op | source)
XLA Modules:
  0.0 235.8 jit_solution(9214345651057739965)
XLA Ops:
  2.2 6.4 %collective-permute-start = (f32[16,64,32]{2,0,1:T(8,128)S(1)}, f32[16,64,32]{2,0,1:T(8,128)S(1)}, u32[]{:S(2)}, u32[]{:S(2)}) collective-permute-start(f32[16,64,32]{2,0,1:T(8,128)S(1)} %get-tuple-element.141), channel_id=1, source_target_pairs={{0,8},{8,16},{16,24},{24,32},{32,40},{40,48},{48,56},{56,64},{64,7... | collective-permute-start | bytes 393224 | tf_op jit(solution)/shard_map/ppermute | solution.py:18
  10.6 8.9 %collective-permute-done = f32[16,64,32]{2,0,1:T(8,128)S(1)} collective-permute-done((f32[16,64,32]{2,0,1:T(8,128)S(1)}, f32[16,64,32]{2,0,1:T(8,128)S(1)}, u32[]{:S(2)}, u32[]{:S(2)}) %collective-permute-start) | collective-permute-done | bytes 131104 | tf_op jit(solution)/shard_map/ppermute | solution.py:18
  19.5 2.6 %collective-permute-done.1 = f32[16,64,32]{2,0,1:T(8,128)S(1)} collective-permute-done((f32[16,64,32]{2,0,1:T(8,128)S(1)}, f32[16,64,32]{2,0,1:T(8,128)S(1)}, u32[]{:S(2)}, u32[]{:S(2)}) %collective-permute-start.1) | collective-permute-done | bytes 131104 | tf_op jit(solution)/shard_map/ppermute | solution.py:21
  22.2 3.1 %collective-permute-start.2 = (f32[16,1,192]{2,0,1:T(8,128)S(1)}, f32[16,1,192]{2,0,1:T(8,128)S(1)}, u32[]{:S(2)}, u32[]{:S(2)}) collective-permute-start(f32[16,1,192]{2,0,1:T(8,128)S(1)} %get-tuple-element.130), channel_id=1, source_target_pairs={{0,1},{1,2},{2,3},{3,4},{4,5},{5,6},{6,7},{8,9},{9,10},{10,11},{11... | collective-permute-start | bytes 36872 | tf_op jit(solution)/shard_map/ppermute | solution.py:18
  25.3 8.4 %collective-permute-start.3 = (f32[16,1,192]{2,0,1:T(8,128)S(1)}, f32[16,1,192]{2,0,1:T(8,128)S(1)}, u32[]{:S(2)}, u32[]{:S(2)}) collective-permute-start(f32[16,1,192]{2,0,1:T(8,128)S(1)} %get-tuple-element.131), channel_id=1, source_target_pairs={{1,0},{2,1},{3,2},{4,3},{5,4},{6,5},{7,6},{9,8},{10,9},{11,10},{12... | collective-permute-start | bytes 36872 | tf_op jit(solution)/shard_map/ppermute | solution.py:21
  35.4 3.9 %multiply_add_fusion.1 = f32[16,64,128]{2,0,1:T(8,128)S(1)} fusion(f32[16,64,128]{2,0,1:T(8,128)S(1)} %get-tuple-element.140, f32[16,65,192]{2,0,1:T(8,128)S(1)} %get-tuple-element.129, f32[16,64,160]{2,0,1:T(8,128)S(1)} %constant_dynamic-update-slice_fusion, f32[16,65,192]{2,0,1:T(8,128)S(1)} %get-tuple-element.128, f32[16]{0:T(128)S(1)} %get-tuple-element.195, ...), kind=kLoop, calls=%fused_computation.251 | loop fusion | flops 7471104 | bytes 12715712 | tf_op jit(solution)/shard_map/add | solution.py:36
  45.4 9.3 %collective-permute-done.4 = f32[16,64,32]{2,0,1:T(8,128)S(1)} collective-permute-done((f32[16,64,32]{2,0,1:T(8,128)S(1)}, f32[16,64,32]{2,0,1:T(8,128)S(1)}, u32[]{:S(2)}, u32[]{:S(2)}) %collective-permute-start.4) | collective-permute-done | bytes 131104 | tf_op jit(solution)/shard_map/ppermute | solution.py:18
  54.7 7.7 %collective-permute-done.5 = f32[16,64,32]{2,0,1:T(8,128)S(1)} collective-permute-done((f32[16,64,32]{2,0,1:T(8,128)S(1)}, f32[16,64,32]{2,0,1:T(8,128)S(1)}, u32[]{:S(2)}, u32[]{:S(2)}) %collective-permute-start.5) | collective-permute-done | bytes 131104 | tf_op jit(solution)/shard_map/ppermute | solution.py:21
  64.4 6.0 %collective-permute-start.7 = (f32[16,1,192]{2,0,1:T(8,128)S(1)}, f32[16,1,192]{2,0,1:T(8,128)S(1)}, u32[]{:S(2)}, u32[]{:S(2)}) collective-permute-start(f32[16,1,192]{2,0,1:T(8,128)S(1)} %get-tuple-element.127), channel_id=1, source_target_pairs={{1,0},{2,1},{3,2},{4,3},{5,4},{6,5},{7,6},{9,8},{10,9},{11,10},{12... | collective-permute-start | bytes 36872 | tf_op jit(solution)/shard_map/ppermute | solution.py:21
  72.2 4.5 %multiply_add_fusion = f32[16,64,128]{2,0,1:T(8,128)S(1)} fusion(f32[16,64,128]{2,0,1:T(8,128)S(1)} %get-tuple-element.203, f32[16,65,192]{2,0,1:T(8,128)S(1)} %get-tuple-element.125, f32[16,65,192]{2,0,1:T(8,128)S(1)} %get-tuple-element.124, f32[16]{0:T(128)S(1)} %get-tuple-element.168, f32[16]{0:T(128)S(1)} %get-tuple-element.169, ...), kind=kLoop, calls=%fused_computation.248 | loop fusion | flops 7995392 | bytes 10749632 | tf_op jit(solution)/shard_map/add | solution.py:36
  78.6 3.0 %multiply_reduce_fusion.18 = (f32[16]{0:T(128)S(1)}, f32[16]{0:T(128)S(1)}, f32[16]{0:T(128)S(1)}, f32[16]{0:T(128)S(1)}, f32[16]{0:T(128)S(1)}, /*index=5*/f32[...) fusion(f32[16,65,192]{2,0,1:T(8,128)S(1)} %get-tuple-element.12, ...), kind=kOutput, calls=%fused_computation.210 | convolution fusion | flops 29884128 | bytes 10487936 | tf_op jit(solution)/shard_map/oc,owt->cwt/dot_general | solution.py:108
  87.5 5.1 %multiply_reduce_fusion.9 = (f32[16]{0:T(128)S(1)}, f32[16]{0:T(128)S(1)}, f32[16]{0:T(128)S(1)}, f32[16]{0:T(128)S(1)}, f32[16]{0:T(128)S(1)}, /*index=5*/f32[1...) fusion(f32[16,64,128]{2,0,1:T(8,128)} %copy-done.3, f32[16,64,32]{2,0,1:T(8,128)} %copy-done.8, ...), kind=kLoop, calls=%fused_computation.201 | loop fusion | flops 3932016 | bytes 1835584 | tf_op jit(solution)/shard_map/reduce_sum | solution.py:55
  97.1 3.8 %collective-permute-done.9 = f32[16,64,32]{2,0,1:T(8,128)} collective-permute-done((f32[16,64,32]{2,0,1:T(8,128)}, f32[16,64,32]{2,0,1:T(8,128)}, u32[]{:S(2)}, u32[]{:S(2)}) %collective-permute-start.9) | collective-permute-done | bytes 131104 | tf_op jit(solution)/shard_map/ppermute | solution.py:21
  103.6 7.6 %collective-permute-start.11 = (f32[16,1,192]{2,0,1:T(8,128)S(1)}, f32[16,1,192]{2,0,1:T(8,128)S(1)}, u32[]{:S(2)}, u32[]{:S(2)}) collective-permute-start(f32[16,1,192]{2,0,1:T(8,128)S(1)} %get-tuple-element.123), channel_id=1, source_target_pairs={{1,0},{2,1},{3,2},{4,3},{5,4},{6,5},{7,6},{9,8},{10,9},{11,10},{12... | collective-permute-start | bytes 36872 | tf_op jit(solution)/shard_map/ppermute | solution.py:21
  116.1 6.5 %fusion.99 = (f32[16]{0:T(128)S(1)}, f32[16,64,128]{2,0,1:T(8,128)S(1)}) fusion(f32[16,64,128]{2,0,1:T(8,128)S(1)} %copy-done.15, f32[16,65,192]{2,0,1:T(8,128)S(1)} %get-tuple-element.121, f32[16]{0:T(128)S(1)} %get-tuple-element.143, f32[16]{0:T(128)S(1)} %get-tuple-element.162, f32[16]{0:T(128)S(1)} %get-tuple-element.167, f32[16]{0:T(128)S(1)} %get-tuple-element.166, ...), kind=kLoop, calls=%fused_computation.333 | loop fusion | flops 9175024 | bytes 11273984 | tf_op jit(solution)/shard_map/reduce_sum | solution.py:115
  123.4 3.0 %multiply_reduce_fusion.45 = (f32[16]{0:T(128)S(1)}, f32[16]{0:T(128)S(1)}, f32[16]{0:T(128)S(1)}, f32[16]{0:T(128)S(1)}, f32[16]{0:T(128)S(1)}, /*index=5*/f32[...) fusion(f32[16,65,192]{2,0,1:T(8,128)S(1)} %get-tuple-element.12, ...), kind=kOutput, calls=%fused_computation.237 | convolution fusion | flops 29884128 | bytes 10487936 | tf_op jit(solution)/shard_map/oc,owt->cwt/dot_general | solution.py:116
  132.5 9.1 %all-gather.5 = f32[4,1,1408]{2,1,0:T(1,128)S(1)} all-gather(f32[1,1,1408]{2,1,0:T(1,128)S(1)} %reshape.68), channel_id=3, replica_groups=mesh['y'=8,'z_hi'=4,'core'=2,'z_lo'=2,'x'=4] {'x'}, dimensions={0}, use_global_device_ids=true | all-gather | bytes 28160 | tf_op jit(solution)/shard_map/all_gather | solution.py:126
  141.6 21.4 %all-gather.6 = f32[8,1,1408]{2,1,0:T(1,128)S(1)} all-gather(f32[1,1,1408]{2,1,0:T(1,128)S(1)} %reshape.70), channel_id=4, replica_groups=mesh['y'=8,'z_hi'=4,'core'=2,'z_lo'=2,'x'=4] {'z_hi','z_lo'}, dimensions={0}, use_global_device_ids=true | all-gather | bytes 50688 | tf_op jit(solution)/shard_map/all_gather | solution.py:126
  163.1 18.3 %all-gather.7 = f32[8,1,1408]{2,1,0:T(1,128)S(1)} all-gather(f32[1,1,1408]{2,1,0:T(1,128)S(1)} %reshape.72), channel_id=5, replica_groups=mesh['y'=8,'z_hi'=4,'core'=2,'z_lo'=2,'x'=4] {'y'}, dimensions={0}, use_global_device_ids=true | all-gather | bytes 50688 | tf_op jit(solution)/shard_map/all_gather | solution.py:126
  181.5 17.5 %collective-permute-start.12 = (f32[16,64,32]{2,0,1:T(8,128)}, f32[16,64,32]{2,0,1:T(8,128)S(1)}, u32[]{:S(2)}, u32[]{:S(2)}) collective-permute-start(f32[16,64,32]{2,0,1:T(8,128)} %get-tuple-element.132), channel_id=1, source_target_pairs={{0,8},{8,16},{16,24},{24,32},{32,40},{40,48},{48,56},{56,64},{64,7... | collective-permute-start | bytes 393224 | tf_op jit(solution)/shard_map/ppermute | solution.py:18
  201.1 9.4 %collective-permute-done.12 = f32[16,64,32]{2,0,1:T(8,128)S(1)} collective-permute-done((f32[16,64,32]{2,0,1:T(8,128)}, f32[16,64,32]{2,0,1:T(8,128)S(1)}, u32[]{:S(2)}, u32[]{:S(2)}) %collective-permute-start.12) | collective-permute-done | bytes 131104 | tf_op jit(solution)/shard_map/ppermute | solution.py:18
  210.5 5.8 %collective-permute-done.13 = f32[16,64,32]{2,0,1:T(8,128)S(1)} collective-permute-done((f32[16,64,32]{2,0,1:T(8,128)}, f32[16,64,32]{2,0,1:T(8,128)S(1)}, u32[]{:S(2)}, u32[]{:S(2)}) %collective-permute-start.13) | collective-permute-done | bytes 131104 | tf_op jit(solution)/shard_map/ppermute | solution.py:21
  218.3 6.3 %collective-permute-start.15 = (f32[16,1,192]{2,0,1:T(8,128)S(1)}, f32[16,1,192]{2,0,1:T(8,128)S(1)}, u32[]{:S(2)}, u32[]{:S(2)}) collective-permute-start(f32[16,1,192]{2,0,1:T(8,128)S(1)} %get-tuple-element.119), channel_id=1, source_target_pairs={{1,0},{2,1},{3,2},{4,3},{5,4},{6,5},{7,6},{9,8},{10,9},{11,10},{12... | collective-permute-start | bytes 36872 | tf_op jit(solution)/shard_map/ppermute | solution.py:21
  230.4 4.5 %fusion.14 = f32[16,64,128]{2,0,1:T(8,128)S(1)} fusion(f32[16,64,128]{2,0,1:T(8,128)S(1)} %get-tuple-element.205, f32[16,64,32]{2,0,1:T(8,128)S(1)} %copy-done.10, f32[16,64,32]{2,0,1:T(8,128)S(1)} %collective-permute-done.12, f32[16,65,192]{2,0,1:T(8,128)S(1)} %get-tuple-element.117, f32[16,65,192]{2,0,1:T(8,128)S(1)} %get-tuple-element.116, ...), kind=kLoop, calls=%fused_computation.70 | loop fusion | flops 7995392 | bytes 10749632 | tf_op jit(solution)/shard_map/add | solution.py:36
  (122 shorter events, 52.6 us)
Async XLA Ops:
  0.6 76.1 %copy-start = (f32[16,16]{1,0:T(8,128)S(1)}, f32[16,16]{1,0:T(8,128)}, u32[]{:S(2)}) copy-start(f32[16,16]{1,0:T(8,128)} %param.13) | copy-start | bytes 3076
  2.0 8.5 %copy-start.17 = (f32[16,3,9]{0,1,2:T(4,128)S(1)}, f32[16,3,9]{0,1,2:T(4,128)}, u32[]{:S(2)}) copy-start(f32[16,3,9]{0,1,2:T(4,128)} %param.9) | copy-start | bytes 5188
  2.2 17.2 %collective-permute-start = (f32[16,64,32]{2,0,1:T(8,128)S(1)}, f32[16,64,32]{2,0,1:T(8,128)S(1)}, u32[]{:S(2)}, u32[]{:S(2)}) collective-permute-start(f32[16,64,32]{2,0,1:T(8,128)S(1)} %get-tuple-element.141), channel_id=1, source_target_pairs={{0,8},{8,16},{16,24},{24,32},{32,40},{40,48},{48,56},{56,64},{64,7... | collective-permute-start | bytes 393224 | tf_op jit(solution)/shard_map/ppermute | solution.py:18
  8.6 13.5 %collective-permute-start.1 = (f32[16,64,32]{2,0,1:T(8,128)S(1)}, f32[16,64,32]{2,0,1:T(8,128)S(1)}, u32[]{:S(2)}, u32[]{:S(2)}) collective-permute-start(f32[16,64,32]{2,0,1:T(8,128)S(1)} %get-tuple-element.142), channel_id=1, source_target_pairs={{8,0},{16,8},{24,16},{32,24},{40,32},{48,40},{56,48},{64,56},{72,6... | collective-permute-start | bytes 393224 | tf_op jit(solution)/shard_map/ppermute | solution.py:21
  19.5 15.9 %copy-start.5 = (f32[16,64,32]{2,0,1:T(8,128)}, f32[16,64,32]{2,0,1:T(8,128)S(1)}, u32[]{:S(2)}) copy-start(f32[16,64,32]{2,0,1:T(8,128)S(1)} %collective-permute-done) | copy-start | bytes 393220
  22.2 11.6 %collective-permute-start.2 = (f32[16,1,192]{2,0,1:T(8,128)S(1)}, f32[16,1,192]{2,0,1:T(8,128)S(1)}, u32[]{:S(2)}, u32[]{:S(2)}) collective-permute-start(f32[16,1,192]{2,0,1:T(8,128)S(1)} %get-tuple-element.130), channel_id=1, source_target_pairs={{0,1},{1,2},{2,3},{3,4},{4,5},{5,6},{6,7},{8,9},{9,10},{10,11},{11... | collective-permute-start | bytes 36872 | tf_op jit(solution)/shard_map/ppermute | solution.py:18
  25.3 9.2 %collective-permute-start.3 = (f32[16,1,192]{2,0,1:T(8,128)S(1)}, f32[16,1,192]{2,0,1:T(8,128)S(1)}, u32[]{:S(2)}, u32[]{:S(2)}) collective-permute-start(f32[16,1,192]{2,0,1:T(8,128)S(1)} %get-tuple-element.131), channel_id=1, source_target_pairs={{1,0},{2,1},{3,2},{4,3},{5,4},{6,5},{7,6},{9,8},{10,9},{11,10},{12... | collective-permute-start | bytes 36872 | tf_op jit(solution)/shard_map/ppermute | solution.py:21
  41.0 13.7 %collective-permute-start.4 = (f32[16,64,32]{2,0,1:T(8,128)S(1)}, f32[16,64,32]{2,0,1:T(8,128)S(1)}, u32[]{:S(2)}, u32[]{:S(2)}) collective-permute-start(f32[16,64,32]{2,0,1:T(8,128)S(1)} %get-tuple-element.137), channel_id=1, source_target_pairs={{0,8},{8,16},{16,24},{24,32},{32,40},{40,48},{48,56},{56,64},{64,7... | collective-permute-start | bytes 393224 | tf_op jit(solution)/shard_map/ppermute | solution.py:18
  43.0 19.4 %collective-permute-start.5 = (f32[16,64,32]{2,0,1:T(8,128)S(1)}, f32[16,64,32]{2,0,1:T(8,128)S(1)}, u32[]{:S(2)}, u32[]{:S(2)}) collective-permute-start(f32[16,64,32]{2,0,1:T(8,128)S(1)} %get-tuple-element.138), channel_id=1, source_target_pairs={{8,0},{16,8},{24,16},{32,24},{40,32},{48,40},{56,48},{64,56},{72,6... | collective-permute-start | bytes 393224 | tf_op jit(solution)/shard_map/ppermute | solution.py:21
  54.7 17.4 %copy-start.7 = (f32[16,64,32]{2,0,1:T(8,128)}, f32[16,64,32]{2,0,1:T(8,128)S(1)}, u32[]{:S(2)}) copy-start(f32[16,64,32]{2,0,1:T(8,128)S(1)} %collective-permute-done.4) | copy-start | bytes 393220
  62.4 9.8 %copy-start.8 = (f32[16,64,32]{2,0,1:T(8,128)}, f32[16,64,32]{2,0,1:T(8,128)S(1)}, u32[]{:S(2)}) copy-start(f32[16,64,32]{2,0,1:T(8,128)S(1)} %collective-permute-done.5) | copy-start | bytes 393220
  62.5 8.0 %collective-permute-start.6 = (f32[16,1,192]{2,0,1:T(8,128)S(1)}, f32[16,1,192]{2,0,1:T(8,128)S(1)}, u32[]{:S(2)}, u32[]{:S(2)}) collective-permute-start(f32[16,1,192]{2,0,1:T(8,128)S(1)} %get-tuple-element.126), channel_id=1, source_target_pairs={{0,1},{1,2},{2,3},{3,4},{4,5},{5,6},{6,7},{8,9},{9,10},{10,11},{11... | collective-permute-start | bytes 36872 | tf_op jit(solution)/shard_map/ppermute | solution.py:18
  64.4 6.9 %collective-permute-start.7 = (f32[16,1,192]{2,0,1:T(8,128)S(1)}, f32[16,1,192]{2,0,1:T(8,128)S(1)}, u32[]{:S(2)}, u32[]{:S(2)}) collective-permute-start(f32[16,1,192]{2,0,1:T(8,128)S(1)} %get-tuple-element.127), channel_id=1, source_target_pairs={{1,0},{2,1},{3,2},{4,3},{5,4},{6,5},{7,6},{9,8},{10,9},{11,10},{12... | collective-permute-start | bytes 36872 | tf_op jit(solution)/shard_map/ppermute | solution.py:21
  82.8 14.3 %collective-permute-start.8 = (f32[16,64,32]{2,0,1:T(8,128)}, f32[16,64,32]{2,0,1:T(8,128)}, u32[]{:S(2)}, u32[]{:S(2)}) collective-permute-start(f32[16,64,32]{2,0,1:T(8,128)} %get-tuple-element.134), channel_id=1, source_target_pairs={{0,8},{8,16},{16,24},{24,32},{32,40},{40,48},{48,56},{56,64},{64,7... | collective-permute-start | bytes 393224 | tf_op jit(solution)/shard_map/ppermute | solution.py:18
  85.3 15.5 %collective-permute-start.9 = (f32[16,64,32]{2,0,1:T(8,128)}, f32[16,64,32]{2,0,1:T(8,128)}, u32[]{:S(2)}, u32[]{:S(2)}) collective-permute-start(f32[16,64,32]{2,0,1:T(8,128)} %get-tuple-element.135), channel_id=1, source_target_pairs={{8,0},{16,8},{24,16},{32,24},{40,32},{48,40},{56,48},{64,56},{72,6... | collective-permute-start | bytes 393224 | tf_op jit(solution)/shard_map/ppermute | solution.py:21
  92.5 8.3 %copy-start.4 = (f32[16,64,128]{2,0,1:T(8,128)S(1)}, f32[16,64,128]{2,0,1:T(8,128)}, u32[]{:S(2)}) copy-start(f32[16,64,128]{2,0,1:T(8,128)} %copy-done.3) | copy-start | bytes 1572868
  101.7 11.9 %collective-permute-start.10 = (f32[16,1,192]{2,0,1:T(8,128)S(1)}, f32[16,1,192]{2,0,1:T(8,128)S(1)}, u32[]{:S(2)}, u32[]{:S(2)}) collective-permute-start(f32[16,1,192]{2,0,1:T(8,128)S(1)} %get-tuple-element.122), channel_id=1, source_target_pairs={{0,1},{1,2},{2,3},{3,4},{4,5},{5,6},{6,7},{8,9},{9,10},{10,11},{11... | collective-permute-start | bytes 36872 | tf_op jit(solution)/shard_map/ppermute | solution.py:18
  103.6 10.0 %collective-permute-start.11 = (f32[16,1,192]{2,0,1:T(8,128)S(1)}, f32[16,1,192]{2,0,1:T(8,128)S(1)}, u32[]{:S(2)}, u32[]{:S(2)}) collective-permute-start(f32[16,1,192]{2,0,1:T(8,128)S(1)} %get-tuple-element.123), channel_id=1, source_target_pairs={{1,0},{2,1},{3,2},{4,3},{5,4},{6,5},{7,6},{9,8},{10,9},{11,10},{12... | collective-permute-start | bytes 36872 | tf_op jit(solution)/shard_map/ppermute | solution.py:21
  116.1 6.5 %copy-start.13 = (f32[16,64,128]{2,0,1:T(8,128)S(1)}, f32[16,64,128]{2,0,1:T(8,128)}, u32[]{:S(2)}) copy-start(f32[16,64,128]{2,0,1:T(8,128)} %copy-done.12) | copy-start | bytes 1572868
  181.5 29.0 %collective-permute-start.12 = (f32[16,64,32]{2,0,1:T(8,128)}, f32[16,64,32]{2,0,1:T(8,128)S(1)}, u32[]{:S(2)}, u32[]{:S(2)}) collective-permute-start(f32[16,64,32]{2,0,1:T(8,128)} %get-tuple-element.132), channel_id=1, source_target_pairs={{0,8},{8,16},{16,24},{24,32},{32,40},{40,48},{48,56},{56,64},{64,7... | collective-permute-start | bytes 393224 | tf_op jit(solution)/shard_map/ppermute | solution.py:18
  199.0 17.3 %collective-permute-start.13 = (f32[16,64,32]{2,0,1:T(8,128)}, f32[16,64,32]{2,0,1:T(8,128)S(1)}, u32[]{:S(2)}, u32[]{:S(2)}) collective-permute-start(f32[16,64,32]{2,0,1:T(8,128)} %get-tuple-element.133), channel_id=1, source_target_pairs={{8,0},{16,8},{24,16},{32,24},{40,32},{48,40},{56,48},{64,56},{72,6... | collective-permute-start | bytes 393224 | tf_op jit(solution)/shard_map/ppermute | solution.py:21
  216.3 11.9 %copy-start.9 = (f32[16,64,32]{2,0,1:T(8,128)}, f32[16,64,32]{2,0,1:T(8,128)S(1)}, u32[]{:S(2)}) copy-start(f32[16,64,32]{2,0,1:T(8,128)S(1)} %collective-permute-done.13) | copy-start | bytes 393220
  216.3 11.9 %collective-permute-start.14 = (f32[16,1,192]{2,0,1:T(8,128)S(1)}, f32[16,1,192]{2,0,1:T(8,128)S(1)}, u32[]{:S(2)}, u32[]{:S(2)}) collective-permute-start(f32[16,1,192]{2,0,1:T(8,128)S(1)} %get-tuple-element.118), channel_id=1, source_target_pairs={{0,1},{1,2},{2,3},{3,4},{4,5},{5,6},{6,7},{8,9},{9,10},{10,11},{11... | collective-permute-start | bytes 36872 | tf_op jit(solution)/shard_map/ppermute | solution.py:18
  218.3 9.9 %collective-permute-start.15 = (f32[16,1,192]{2,0,1:T(8,128)S(1)}, f32[16,1,192]{2,0,1:T(8,128)S(1)}, u32[]{:S(2)}, u32[]{:S(2)}) collective-permute-start(f32[16,1,192]{2,0,1:T(8,128)S(1)} %get-tuple-element.119), channel_id=1, source_target_pairs={{1,0},{2,1},{3,2},{4,3},{5,4},{6,5},{7,6},{9,8},{10,9},{11,10},{12... | collective-permute-start | bytes 36872 | tf_op jit(solution)/shard_map/ppermute | solution.py:21
  (15 other events, 45.2 us)
